TPU v7x, 32 devices: a whole 2x2x4 slice. The times are simulated.
32 devices in a mesh: tgt: 4 (over y, x), sup: 8 (over z, core).
Axes of the slice: x: 2, y: 2, z: 4, core: 2. Of those that a mesh axis runs over, the one named last changes fastest.
Arguments:
- support: float32 [32, 3, 1024], P(('sup', 'tgt')), may hold values from -14 to 14
- coeffs: float32 [32, 100], P('sup'), may hold values from -10 to 10
- targets: float32 [32, 3, 1024], P(('tgt', 'sup')), may hold values from -14 to 14
- labels: float32 [32, 100], P(('tgt', 'sup')), may hold values from -5 to 5
Outputs:
- support_grad: float32 [32, 3, 1024], P(('sup', 'tgt'))
- residual: float32 [32, 100], P(('tgt', 'sup'))
All inputs are finite; a program needn't handle non-finite values.
Results may differ from a plain program's by a relative error of at most 0.000064.
Values sent between devices are 32-bit elements; how exact they have to be, the bound alone decides.
No kernel may reach another device: no remote copies, remote signals or barrier semaphores. Data moves between devices by JAX's collectives and lax.ppermute only.
A program may use at most 128 MiB of HBM per device.

v0:
```python
import math
import jax
import jax.numpy as jnp
from jax import lax
from jax.sharding import PartitionSpec as P

SIDE = 32
DEPTH = 3
WEIGHT_VAR = 1.6
BIAS_VAR = 0.1


def spread(values):
    side_cells = values.shape[0]
    padded = jnp.pad(values, ((1, 1), (1, 1), (0, 0)))
    summed = jnp.zeros_like(values)
    for row_shift in range(3):
        for col_shift in range(3):
            summed = (
                summed
                + padded[row_shift : row_shift + side_cells, col_shift : col_shift + side_cells]
            )
    return summed / 9.0


def self_levels(images):
    image_count = images.shape[0]
    energy = jnp.mean(images * images, axis=1)
    kernel_level = WEIGHT_VAR * spread(energy.T.reshape(SIDE, SIDE, image_count)) + BIAS_VAR
    levels = [kernel_level]
    for layer_idx in range(DEPTH - 1):
        activated = 2.0 / math.pi * jnp.arcsin(2.0 * kernel_level / (1.0 + 2.0 * kernel_level))
        kernel_level = WEIGHT_VAR * spread(activated) + BIAS_VAR
        levels.append(kernel_level)
    return levels


def pair_kernel(support, targets):
    sup_count = support.shape[0]
    tgt_count = targets.shape[0]
    sup_levels = self_levels(support)
    tgt_levels = self_levels(targets)
    products = (
        jnp.einsum("scp,tcp->pst", support, targets, precision=lax.Precision.HIGHEST)
        / support.shape[1]
    )
    kernel_level = (
        WEIGHT_VAR * spread(products.reshape(SIDE, SIDE, sup_count * tgt_count)) + BIAS_VAR
    )
    activated = kernel_level
    for layer_idx in range(DEPTH):
        sup_gain = lax.rsqrt(1.0 + 2.0 * sup_levels[layer_idx])
        tgt_gain = lax.rsqrt(1.0 + 2.0 * tgt_levels[layer_idx])
        correlation = (
            2.0
            * kernel_level.reshape(SIDE, SIDE, sup_count, tgt_count)
            * sup_gain[:, :, :, None]
            * tgt_gain[:, :, None, :]
        )
        activated = 2.0 / math.pi * jnp.arcsin(correlation)
        if layer_idx + 1 < DEPTH:
            kernel_level = (
                WEIGHT_VAR * spread(activated.reshape(SIDE, SIDE, sup_count * tgt_count)) + BIAS_VAR
            )
    return WEIGHT_VAR * jnp.mean(activated, axis=(0, 1)) + BIAS_VAR


def product(left, right):
    return jnp.dot(left, right, precision=lax.Precision.HIGHEST, preferred_element_type=jnp.float32)


def local(support, coeffs, targets, labels):
    tgt_dev = targets.shape[0]
    block = lax.all_gather(support, "tgt", axis=0, tiled=True)
    group, group_labels = (
        lax.all_gather(targets, "sup", axis=0, tiled=True),
        lax.all_gather(labels, "sup", axis=0, tiled=True),
    )
    theta, pullback = jax.vjp(lambda images: pair_kernel(images, group), block)
    predicted = lax.psum(product(theta.T, coeffs), "sup")
    misfit = predicted - group_labels
    residual = lax.dynamic_slice_in_dim(misfit, lax.axis_index("sup") * tgt_dev, tgt_dev, 0)
    block_grad = pullback(product(coeffs, misfit.T))[0]
    support_grad = lax.psum_scatter(block_grad, "tgt", scatter_dimension=0, tiled=True)
    return (support_grad, residual)


def solution(mesh):
    return jax.shard_map(
        local,
        mesh=mesh,
        in_specs=(
            P(("sup", "tgt"), None, None),
            P("sup", None),
            P(("tgt", "sup"), None, None),
            P(("tgt", "sup"), None),
        ),
        out_specs=(P(("sup", "tgt"), None, None), P(("tgt", "sup"), None)),
        check_vma=False,
    )
```

profile of v0, /device:TPU:0, one launch (start us, length us, event | category | flops | bytes accessed | tf_op | source)
XLA Modules:
  0.0 127.9 jit_solution(11291109133535098446)
XLA Ops:
  0.7 0.7 copy.146
  1.4 9.7 %all_gather.9 = f32[4,3,1024]{2,1,0:T(4,128)S(1)} all-gather(f32[1,3,1024]{2,1,0:T(4,128)S(1)} %copy.146), channel_id=1, replica_groups=mesh['tgt'=4,'sup'=8] {'tgt'}, dimensions={0}, use_global_device_ids=true | all-gather | bytes 61440 | tf_op jit(solution)/shard_map/all_gather | solution.py:74
  12.0 14.3 %all_gather.10 = f32[8,3,1024]{2,1,0:T(4,128)S(1)} all-gather(f32[1,3,1024]{2,1,0:T(4,128)S(1)} %copy.147), channel_id=1, replica_groups=mesh['tgt'=4,'sup'=8] {'sup'}, dimensions={0}, use_global_device_ids=true | all-gather | bytes 110592 | tf_op jit(solution)/shard_map/all_gather | solution.py:76
  26.8 0.9 add_rsqrt_fusion.1
  27.9 2.7 %copy.149 = f32[8,3,1024]{1,0,2:T(8,128)} copy(f32[8,3,1024]{2,1,0:T(4,128)S(1)} %all_gather.10) | data formatting | bytes 196608 | tf_op jit(solution)/shard_map/all_gather | solution.py:76
  30.6 1.8 %copy.148 = f32[4,3,1024]{1,0,2:T(4,128)} copy(f32[4,3,1024]{2,1,0:T(4,128)S(1)} %all_gather.9) | data formatting | bytes 98304 | tf_op jit(solution)/shard_map/all_gather | solution.py:74
  32.4 9.7 %convolution_multiply_fusion = f32[1024,4,8]{2,1,0:T(4,128)S(1)} fusion(f32[4,3,1024]{1,0,2:T(4,128)} %copy.148, f32[8,3,1024]{1,0,2:T(8,128)} %copy.149), kind=kOutput, calls=%fused_computation | convolution fusion | flops 1212416 | bytes 278528 | tf_op jit(solution)/shard_map/jvp(scp,tcp->pst)/dot_general | solution.py:44
  42.1 0.9 copy.150
  43.2 2.7 %add_multiply_fusion.3 = (f32[32,32,32]{1,0,2:T(8,128)S(1)}, f32[32,32,32]{1,0,2:T(8,128)S(1)}) fusion(f32[32,32,32]{1,2,0:T(8,128)S(1)} %get-tuple-element.40, f32[32,32,32]{1,2,0:T(8,128)S(1)} %get-tuple-element.41, f32[32,32,32]{1,0,2:T(8,128)S(1)} %reshape.78), kind=kLoop, calls=%fused_computation.116 | loop fusion | flops 589824 | bytes 655360 | tf_op jit(solution)/shard_map/jvp()/mul | solution.py:60
  45.9 0.7 add_multiply_fusion.11
  47.7 3.3 %add_multiply_fusion.1 = (f32[32,32,32]{1,0,2:T(8,128)S(1)}, f32[32,32,32]{1,0,2:T(8,128)}) fusion(f32[32,32,32]{1,2,0:T(8,128)S(1)} %get-tuple-element.42, f32[32,32,32]{1,2,0:T(8,128)S(1)} %get-tuple-element.43, f32[32,32,32]{1,0,2:T(8,128)S(1)} %get-tuple-element.26), kind=kLoop, calls=%fused_computation.114 | loop fusion | flops 589824 | bytes 655360 | tf_op jit(solution)/shard_map/jvp()/mul | solution.py:60
  51.0 0.7 add_multiply_fusion.9
  51.7 0.8 broadcast_multiply_fusion.2
  53.4 2.3 %multiply_reduce_fusion = (f32[32]{0:T(128)S(1)}, f32[32,32,32]{1,0,2:T(8,128)S(1)}) fusion(f32[32,32,32]{1,2,0:T(8,128)S(1)} %get-tuple-element.44, f32[32,32,32]{1,2,0:T(8,128)S(1)} %get-tuple-element.45, f32[32,32,32]{1,0,2:T(8,128)S(1)} %get-tuple-element.22), kind=kLoop, calls=%fused_computation.112 | loop fusion | flops 622560 | bytes 524416 | tf_op jit(solution)/shard_map/jvp()/reduce_sum | solution.py:65
  55.9 16.9 %psum.7 = f32[8,100]{1,0:T(8,128)S(1)} all-reduce(f32[8,100]{1,0:T(8,128)S(1)} %fusion.155), channel_id=1, replica_groups=mesh['tgt'=4,'sup'=8] {'sup'}, use_global_device_ids=true, to_apply=%region_3.4 | all-reduce | flops 800 | bytes 6400 | tf_op jit(solution)/shard_map/psum | solution.py:80
  72.8 8.6 %all-gather = f32[8,1,100]{2,1,0:T(1,128)S(1)} all-gather(f32[1,1,100]{2,1,0:T(1,128)S(1)} %bitcast.95), channel_id=1, replica_groups=mesh['tgt'=4,'sup'=8] {'sup'}, dimensions={0}, use_global_device_ids=true | all-gather | bytes 3600 | tf_op jit(solution)/shard_map/all_gather | solution.py:77
  81.6 1.4 %fusion.35 = f32[32,32,4]{1,2,0:T(4,128)S(1)} fusion(f32[32,32,32]{1,0,2:T(8,128)S(1)} %get-tuple-element.19, f32[4,8]{1,0:T(4,128)S(1)} %fusion, f32[32,32,8]{1,2,0:T(8,128)S(1)} %copy.169, f32[32,32,4]{1,2,0:T(4,128)} %copy-done.16), kind=kLoop, calls=%fused_computation.84 | loop fusion | flops 323584 | bytes 196736 | tf_op jit(solution)/shard_map/transpose(jvp())/reduce_sum | solution.py:55
  83.0 0.9 fusion.144
  83.9 0.9 broadcast_bitcast_fusion.2
  84.8 2.3 %fusion.47 = f32[32,32,32]{1,0,2:T(8,128)S(1)} fusion(f32[32,32,32]{1,2,0:T(8,128)} %broadcast_bitcast_fusion.2, f32[32,32,32]{1,2,0:T(8,128)S(1)} %get-tuple-element.44, f32[32]{0:T(128)S(1)} %broadcast_in_dim.16, f32[32,32,32]{1,0,2:T(8,128)S(1)} %get-tuple-element.19, f32[32,32,32]{1,2,0:T(8,128)S(1)} %get-tuple-element.45), kind=kLoop, calls=%fused_computation.105 | loop fusion | flops 294912 | bytes 655488 | tf_op jit(solution)/shard_map/transpose(jvp())/div | solution.py:23
  87.7 1.4 %fusion.46 = (f32[32,32,32]{1,0,2:T(8,128)S(1)}, f32[32,32,32]{1,0,2:T(8,128)S(1)}) fusion(f32[32,32,32]{1,2,0:T(8,128)S(1)} %broadcast_bitcast_fusion.1, f32[32,32,32]{1,2,0:T(8,128)S(1)} %copy-done.3, f32[32,32,32]{1,0,2:T(8,128)S(1)} %copy-done.1, f32[32,32,32]{1,2,0:T(8,128)S(1)} %copy-done.5, f32[32,32,32]{1,0,2:T(8,128)S(1)} %fusion.47, ...), kind=kLoop, calls=%fused_computation.103 | loop fusion | flops 524288 | bytes 1048576 | tf_op jit(solution)/shard_map/transpose(jvp())/div | solution.py:23
  89.7 1.5 %fusion.45 = (f32[32,32,32]{1,0,2:T(8,128)S(1)}, f32[32,32,32]{1,0,2:T(8,128)S(1)}) fusion(f32[32,32,32]{1,2,0:T(8,128)S(1)} %broadcast_bitcast_fusion, f32[32,32,32]{1,2,0:T(8,128)S(1)} %get-tuple-element.40, f32[32,32,32]{1,0,2:T(8,128)S(1)} %get-tuple-element.27, f32[32,32,32]{1,2,0:T(8,128)S(1)} %get-tuple-element.41, ...), kind=kLoop, calls=%fused_computation.101 | loop fusion | flops 524288 | bytes 1048576 | tf_op jit(solution)/shard_map/transpose(jvp())/div | solution.py:23
  91.2 0.8 fusion.43
  92.1 0.8 fusion.39
  94.3 0.8 fusion.31
  95.3 1.1 copy.180
  96.4 11.1 %fusion.156 = f32[1024,4,3]{1,2,0:T(4,128)} fusion(f32[1024,4,8]{2,1,0:T(4,128)S(1)} %copy.180, f32[8,3,1024]{1,0,2:T(8,128)} %copy.149), kind=kOutput, calls=%fused_computation.323 | convolution fusion | flops 1179648 | bytes 278528 | tf_op jit(solution)/shard_map/transpose(jvp(scp,tcp->pst))/dot_general | solution.py:44
  107.5 1.8 %copy.182 = f32[1024,4,3]{0,1,2:T(4,128)S(1)} copy(f32[1024,4,3]{1,2,0:T(4,128)} %fusion.156) | data formatting | bytes 98304 | tf_op jit(solution)/shard_map/transpose(jvp(scp,tcp->pst))/dot_general | solution.py:44
  109.5 16.1 %all-reduce.63 = f32[4,3,1024]{2,1,0:T(4,128)S(1)} all-reduce(f32[4,3,1024]{2,1,0:T(4,128)S(1)} %copy.192), channel_id=2, replica_groups=mesh['tgt'=4,'sup'=8] {'tgt'}, use_global_device_ids=true, to_apply=%region_7.8.clone | all-reduce | flops 12288 | bytes 98304
  125.5 0.6 dynamic-slice
  126.1 0.7 constant_dynamic-slice_fusion
  126.8 0.6 copy.193
  (96 shorter events, 7.3 us)
Async XLA Ops:
  0.6 55.1 %copy-start = (f32[4,100]{1,0:T(4,128)S(1)}, f32[4,100]{1,0:T(4,128)}, u32[]{:S(2)}) copy-start(f32[4,100]{1,0:T(4,128)} %param.5) | copy-start | bytes 4804
  0.6 11.3 %copy-start.20 = (f32[1,3,1024]{2,0,1:T(1,128)S(1)}, f32[1,3,1024]{2,0,1:T(1,128)}, u32[]{:S(2)}) copy-start(f32[1,3,1024]{2,0,1:T(1,128)} %param.6) | copy-start | bytes 36868
  11.1 19.5 %copy-start.6 = (f32[4,3,1024]{2,1,0:T(4,128)}, f32[4,3,1024]{2,1,0:T(4,128)S(1)}, u32[]{:S(2)}) copy-start(f32[4,3,1024]{2,1,0:T(4,128)S(1)} %all_gather.9) | copy-start | bytes 147460
  11.9 34.0 %copy-start.8 = (f32[32,32,4]{1,0,2:T(8,128)}, f32[32,32,4]{1,0,2:T(8,128)S(1)}, u32[]{:S(2)}) copy-start(f32[32,32,4]{1,0,2:T(8,128)S(1)} %get-tuple-element.29) | copy-start | bytes 49156
  12.0 15.9 %copy-start.12 = (f32[32,32,4]{1,2,0:T(4,128)}, f32[32,32,4]{1,2,0:T(4,128)S(1)}, u32[]{:S(2)}) copy-start(f32[32,32,4]{1,2,0:T(4,128)S(1)} %copy.155) | copy-start | bytes 49156
  43.0 3.9 %copy-start.17 = (f32[32,32,8]{1,0,2:T(8,128)S(1)}, f32[32,32,8]{1,0,2:T(8,128)}, u32[]{:S(2)}) copy-start(f32[32,32,8]{1,0,2:T(8,128)} %get-tuple-element.31) | copy-start | bytes 98308
  46.8 4.2 %copy-start.10 = (f32[32,32,4]{1,0,2:T(8,128)}, f32[32,32,4]{1,0,2:T(8,128)S(1)}, u32[]{:S(2)}) copy-start(f32[32,32,4]{1,0,2:T(8,128)S(1)} %get-tuple-element.25) | copy-start | bytes 49156
  46.9 4.1 %copy-start.14 = (f32[32,32,4]{1,2,0:T(4,128)}, f32[32,32,4]{1,2,0:T(4,128)S(1)}, u32[]{:S(2)}) copy-start(f32[32,32,4]{1,2,0:T(4,128)S(1)} %copy.163) | copy-start | bytes 49156
  47.7 5.7 %copy-start.2 = (f32[32,32,32]{1,2,0:T(8,128)}, f32[32,32,32]{1,2,0:T(8,128)S(1)}, u32[]{:S(2)}) copy-start(f32[32,32,32]{1,2,0:T(8,128)S(1)} %get-tuple-element.42) | copy-start | bytes 393220
  47.7 5.7 %copy-start.4 = (f32[32,32,32]{1,2,0:T(8,128)}, f32[32,32,32]{1,2,0:T(8,128)S(1)}, u32[]{:S(2)}) copy-start(f32[32,32,32]{1,2,0:T(8,128)S(1)} %get-tuple-element.43) | copy-start | bytes 393220
  52.6 3.1 %copy-start.16 = (f32[32,32,4]{1,2,0:T(4,128)}, f32[32,32,4]{1,2,0:T(4,128)S(1)}, u32[]{:S(2)}) copy-start(f32[32,32,4]{1,2,0:T(4,128)S(1)} %copy.167) | copy-start | bytes 49156
  52.6 20.2 %copy-start.21 = (f32[1,100]{1,0:T(1,128)S(1)}, f32[1,100]{1,0:T(1,128)}, u32[]{:S(2)}) copy-start(f32[1,100]{1,0:T(1,128)} %param.7) | copy-start | bytes 1204
  83.9 3.6 %copy-start.19 = (f32[32,32,4]{1,0,2:T(8,128)S(1)}, f32[32,32,4]{1,0,2:T(8,128)}, u32[]{:S(2)}) copy-start(f32[32,32,4]{1,0,2:T(8,128)} %get-tuple-element.37) | copy-start | bytes 49156
  84.8 2.8 %copy-start.1 = (f32[32,32,32]{1,0,2:T(8,128)S(1)}, f32[32,32,32]{1,0,2:T(8,128)}, u32[]{:S(2)}) copy-start(f32[32,32,32]{1,0,2:T(8,128)} %get-tuple-element.23) | copy-start | bytes 393220
  84.8 2.8 %copy-start.3 = (f32[32,32,32]{1,2,0:T(8,128)S(1)}, f32[32,32,32]{1,2,0:T(8,128)}, u32[]{:S(2)}) copy-start(f32[32,32,32]{1,2,0:T(8,128)} %copy-done.2) | copy-start | bytes 393220
  84.8 2.8 %copy-start.5 = (f32[32,32,32]{1,2,0:T(8,128)S(1)}, f32[32,32,32]{1,2,0:T(8,128)}, u32[]{:S(2)}) copy-start(f32[32,32,32]{1,2,0:T(8,128)} %copy-done.4) | copy-start | bytes 393220
  87.7 1.9 %copy-start.18 = (f32[32,32,4]{1,0,2:T(8,128)S(1)}, f32[32,32,4]{1,0,2:T(8,128)}, u32[]{:S(2)}) copy-start(f32[32,32,4]{1,0,2:T(8,128)} %get-tuple-element.39) | copy-start | bytes 49156
  89.7 1.6 %copy-start.13 = (f32[32,32,4]{1,2,0:T(4,128)S(1)}, f32[32,32,4]{1,2,0:T(4,128)}, u32[]{:S(2)}) copy-start(f32[32,32,4]{1,2,0:T(4,128)} %copy-done.12) | copy-start | bytes 49156
  89.7 2.4 %copy-start.15 = (f32[32,32,4]{1,2,0:T(4,128)S(1)}, f32[32,32,4]{1,2,0:T(4,128)}, u32[]{:S(2)}) copy-start(f32[32,32,4]{1,2,0:T(4,128)} %copy-done.14) | copy-start | bytes 49156
  91.2 1.8 %copy-start.11 = (f32[32,32,4]{1,0,2:T(8,128)S(1)}, f32[32,32,4]{1,0,2:T(8,128)}, u32[]{:S(2)}) copy-start(f32[32,32,4]{1,0,2:T(8,128)} %copy-done.10) | copy-start | bytes 49156
  91.2 2.1 %copy-start.9 = (f32[32,32,4]{1,0,2:T(8,128)S(1)}, f32[32,32,4]{1,0,2:T(8,128)}, u32[]{:S(2)}) copy-start(f32[32,32,4]{1,0,2:T(8,128)} %copy-done.8) | copy-start | bytes 49156
  107.5 1.8 %copy-start.7 = (f32[4,3,1024]{2,1,0:T(4,128)S(1)}, f32[4,3,1024]{2,1,0:T(4,128)}, u32[]{:S(2)}) copy-start(f32[4,3,1024]{2,1,0:T(4,128)} %copy-done.6) | copy-start | bytes 147460
  107.5 18.0 %copy-start.22 = (u32[32]{0:T(128)S(1)}, u32[32]{0:T(128)}, u32[]{:S(2)}) copy-start(u32[32]{0:T(128)} %constant.232) | copy-start | bytes 388
where the time goes:
time: 128 us
  blocking collectives  65.5 us (51%)
  other arithmetic  25.1 us (20%)
  matrix products  21.2 us (17%)
  local copies, waits for them, and re-layouts  14.8 us (12%)
    dot_general x2, matrix products, pair_kernel(): jnp.einsum('scp,tcp->pst', support, targets, precision=lax.Precision.HIGH...  20.9 us
    psum x1, blocking collectives, local(): predicted = lax.psum(product(theta.T, coeffs), 'sup')  16.9 us
    unnamed x1, blocking collectives  16.1 us
    all_gather x1, blocking collectives, local(): lax.all_gather(targets, 'sup', axis=0, tiled=True)  14.3 us
    all_gather x1, blocking collectives, local(): block = lax.all_gather(support, 'tgt', axis=0, tiled=True)  9.71 us
    all_gather x1, blocking collectives, local(): lax.all_gather(labels, 'sup', axis=0, tiled=True)  8.65 us
    div x6, other arithmetic, spread(): return summed / 9.0  6.42 us
    mul x2, other arithmetic, pair_kernel(): activated = 2.0 / math.pi * jnp.arcsin(correlation)  6 us

commit v1 on v0

--- a/solution.py
+++ b/solution.py
@@ -1,3 +1,4 @@
+import functools
 import math
 import jax
 import jax.numpy as jnp
@@ -8,6 +9,14 @@
 DEPTH = 3
 WEIGHT_VAR = 1.6
 BIAS_VAR = 0.1
+
+
+def name_rounds(content, device_axis, k_dim):
+    a_next = jnp.concatenate([content for _ in range(jax.lax.axis_size(device_axis))], axis=k_dim)
+    return jax.lax.all_to_all(a_next, device_axis, k_dim, k_dim, tiled=True)
+
+
+enter_squares_on_mesh = functools.partial(name_rounds, device_axis="sup", k_dim=0)
 
 
 def spread(values):
@@ -74,7 +83,7 @@
     block = lax.all_gather(support, "tgt", axis=0, tiled=True)
     group, group_labels = (
         lax.all_gather(targets, "sup", axis=0, tiled=True),
-        lax.all_gather(labels, "sup", axis=0, tiled=True),
+        enter_squares_on_mesh(labels),
     )
     theta, pullback = jax.vjp(lambda images: pair_kernel(images, group), block)
     predicted = lax.psum(product(theta.T, coeffs), "sup")

time: 128 us -> 127 us (level)
  blocking collectives: 65.5 us -> 53.9 us
  starting transfers between devices: 0 us -> 6.35 us
  local copies, waits for them, and re-layouts: 14.8 us -> 20.6 us
  other arithmetic: 25.1 us -> 23.2 us
    all_gather x1 -> x0, blocking collectives: 8.65 us -> none  [local(): lax.all_gather(labels, 'sup', axis=0, tiled=True)]
    all_to_all x0 -> x1, starting transfers between devices: none -> 6.35 us  [name_rounds(): return jax.lax.all_to_all(a_next, device_axis, k_dim, k_dim, tiled=True)]
    psum x1, blocking collectives: 16.9 us -> 15 us  [local(): predicted = lax.psum(product(theta.T, coeffs), 'sup')]
    rsqrt x3, local copies, waits for them, and re-layouts: 0.14 us -> 1.82 us  [pair_kernel(): sup_gain = lax.rsqrt(1.0 + 2.0 * sup_levels[layer_idx])]
    all_gather x1, blocking collectives: 9.71 us -> 8.24 us  [local(): block = lax.all_gather(support, 'tgt', axis=0, tiled=True)]
    mul x9, local copies, waits for them, and re-layouts: 1.35 us -> 2.79 us  [pair_kernel(): 2.0 * kernel_level.reshape(SIDE, SIDE, sup_count, tgt_count)]
    div x6, other arithmetic: 6.42 us -> 5.12 us  [spread(): return summed / 9.0]
    unnamed x53 -> x47, local copies, waits for them, and re-layouts: 3.1 us -> 4.3 us
  transfers between devices with their start and end apart: 0 -> 1, of which waited for: 0 -> 0; matrix products, arithmetic and copies ran while one was open for 0% -> 28% of each run, Pallas kernels for 0% -> 0%
where the time goes in v1:
time: 127 us
  blocking collectives  53.9 us (42%)
  other arithmetic  23.2 us (18%)
  matrix products  21.2 us (17%)
  local copies, waits for them, and re-layouts  20.6 us (16%)
  starting transfers between devices  6.35 us (5%)
    dot_general x2, matrix products, pair_kernel(): jnp.einsum('scp,tcp->pst', support, targets, precision=lax.Precision.HIGH...  20.8 us
    unnamed x1, blocking collectives  16.2 us
    psum x1, blocking collectives, local(): predicted = lax.psum(product(theta.T, coeffs), 'sup')  15 us
    all_gather x1, blocking collectives, local(): lax.all_gather(targets, 'sup', axis=0, tiled=True)  14.5 us
    all_gather x1, blocking collectives, local(): block = lax.all_gather(support, 'tgt', axis=0, tiled=True)  8.24 us
    all_to_all x1, starting transfers between devices, name_rounds(): return jax.lax.all_to_all(a_next, device_axis, k_dim, k_dim, tiled=True)  6.35 us
    mul x2, other arithmetic, pair_kernel(): activated = 2.0 / math.pi * jnp.arcsin(correlation)  5.96 us
    div x6, other arithmetic, spread(): return summed / 9.0  5.12 us
  transfers between devices with their start and end apart: 1, of which 0 were waited for; matrix products, arithmetic and copies ran while one was open for 28% of the time, Pallas kernels for 0%

profile of v1, /device:TPU:0, one launch (start us, length us, event | category | flops | bytes accessed | tf_op | source)
XLA Modules:
  0.0 126.5 jit_solution(16598067106635339634)
XLA Ops:
  0.6 1.3 concatenate.3
  1.9 6.4 %all-to-all-start = ((f32[8,1,100]{2,1,0:T(1,128)}), f32[8,1,100]{2,1,0:T(1,128)S(1)}, u32[]{:S(2)}, u32[]{:S(2)}) async-start(f32[8,1,100]{2,1,0:T(1,128)} %concatenate.3), calls=%async_computation | async-start | bytes 8192 | tf_op jit(solution)/shard_map/all_to_all | solution.py:16
  9.0 14.5 %all_gather.7 = f32[8,3,1024]{2,1,0:T(4,128)S(1)} all-gather(f32[1,3,1024]{2,1,0:T(4,128)S(1)} %copy.144), channel_id=1, replica_groups=mesh['tgt'=4,'sup'=8] {'sup'}, dimensions={0}, use_global_device_ids=true | all-gather | bytes 110592 | tf_op jit(solution)/shard_map/all_gather | solution.py:85
  23.5 2.7 %copy.146 = f32[8,3,1024]{1,0,2:T(8,128)} copy(f32[8,3,1024]{2,1,0:T(4,128)S(1)} %all_gather.7) | data formatting | bytes 196608 | tf_op jit(solution)/shard_map/all_gather | solution.py:85
  26.2 8.2 %all_gather.6 = f32[4,3,1024]{2,1,0:T(4,128)S(1)} all-gather(f32[1,3,1024]{2,1,0:T(4,128)S(1)} %copy.143), channel_id=1, replica_groups=mesh['tgt'=4,'sup'=8] {'tgt'}, dimensions={0}, use_global_device_ids=true | all-gather | bytes 61440 | tf_op jit(solution)/shard_map/all_gather | solution.py:83
  35.1 0.9 copy.145
  38.3 9.7 %convolution_multiply_fusion = f32[1024,4,8]{2,1,0:T(4,128)} fusion(f32[4,3,1024]{1,0,2:T(4,128)S(1)} %copy.145, f32[8,3,1024]{1,0,2:T(8,128)} %copy.146), kind=kOutput, calls=%fused_computation | convolution fusion | flops 1212416 | bytes 278528 | tf_op jit(solution)/shard_map/jvp(scp,tcp->pst)/dot_general | solution.py:53
  48.0 2.0 %copy.147 = f32[1024,4,8]{0,2,1:T(8,128)S(1)} copy(f32[1024,4,8]{2,1,0:T(4,128)} %convolution_multiply_fusion) | data formatting | bytes 262144 | tf_op jit(solution)/shard_map/jvp()/div | solution.py:53
  50.2 0.7 add_multiply_fusion.11
  51.8 0.8 add_multiply_fusion.9
  52.6 0.8 broadcast_multiply_fusion.2
  54.4 3.3 %add_multiply_fusion.3 = (f32[32,32,32]{1,0,2:T(8,128)S(1)}, f32[32,32,32]{1,0,2:T(8,128)}) fusion(f32[32,32,32]{1,2,0:T(8,128)S(1)} %get-tuple-element.40, f32[32,32,32]{1,2,0:T(8,128)S(1)} %get-tuple-element.41, f32[32,32,32]{1,0,2:T(8,128)S(1)} %reshape.85), kind=kLoop, calls=%fused_computation.116 | loop fusion | flops 589824 | bytes 655360 | tf_op jit(solution)/shard_map/jvp()/mul | solution.py:69
  57.8 2.7 %add_multiply_fusion.1 = (f32[32,32,32]{1,0,2:T(8,128)S(1)}, f32[32,32,32]{1,0,2:T(8,128)S(1)}) fusion(f32[32,32,32]{1,2,0:T(8,128)S(1)} %get-tuple-element.42, f32[32,32,32]{1,2,0:T(8,128)S(1)} %get-tuple-element.43, f32[32,32,32]{1,0,2:T(8,128)S(1)} %get-tuple-element.26), kind=kLoop, calls=%fused_computation.114 | loop fusion | flops 589824 | bytes 655360 | tf_op jit(solution)/shard_map/jvp()/mul | solution.py:69
  60.4 2.3 %multiply_reduce_fusion = (f32[32]{0:T(128)S(1)}, f32[32,32,32]{1,0,2:T(8,128)S(1)}) fusion(f32[32,32,32]{1,2,0:T(8,128)S(1)} %get-tuple-element.44, f32[32,32,32]{1,2,0:T(8,128)S(1)} %get-tuple-element.45, f32[32,32,32]{1,0,2:T(8,128)S(1)} %get-tuple-element.22), kind=kLoop, calls=%fused_computation.112 | loop fusion | flops 622560 | bytes 524416 | tf_op jit(solution)/shard_map/jvp()/reduce_sum | solution.py:74
  62.8 0.9 copy.172
  63.7 0.9 broadcast_bitcast_fusion.1
  64.5 0.9 copy.175
  65.4 0.9 broadcast_bitcast_fusion
  66.5 1.2 dynamic-slice
  67.7 15.0 %psum.7 = f32[8,100]{1,0:T(8,128)S(1)} all-reduce(f32[8,100]{1,0:T(8,128)S(1)} %fusion.155), channel_id=1, replica_groups=mesh['tgt'=4,'sup'=8] {'sup'}, use_global_device_ids=true, to_apply=%region_3.4 | all-reduce | flops 800 | bytes 6400 | tf_op jit(solution)/shard_map/psum | solution.py:89
  83.0 1.4 %fusion.35 = f32[32,32,4]{1,2,0:T(4,128)S(1)} fusion(f32[32,32,32]{1,0,2:T(8,128)S(1)} %get-tuple-element.19, f32[4,8]{1,0:T(4,128)S(1)} %fusion, f32[32,32,8]{1,2,0:T(8,128)S(1)} %copy.166, f32[32,32,4]{1,2,0:T(4,128)} %copy-done.18), kind=kLoop, calls=%fused_computation.84 | loop fusion | flops 323584 | bytes 196736 | tf_op jit(solution)/shard_map/transpose(jvp())/reduce_sum | solution.py:64
  84.3 0.9 fusion.144
  85.4 0.9 fusion.47
  86.8 1.5 %fusion.46 = (f32[32,32,32]{1,0,2:T(8,128)S(1)}, f32[32,32,32]{1,0,2:T(8,128)S(1)}) fusion(f32[32,32,32]{1,2,0:T(8,128)S(1)} %copy-done.7, f32[32,32,32]{1,2,0:T(8,128)S(1)} %copy-done.3, f32[32,32,32]{1,0,2:T(8,128)S(1)} %get-tuple-element.23, f32[32,32,32]{1,2,0:T(8,128)S(1)} %copy-done.5, f32[32,32,32]{1,0,2:T(8,128)S(1)} %fusion.47, ...), kind=kLoop, calls=%fused_computation.103 | loop fusion | flops 524288 | bytes 1048576 | tf_op jit(solution)/shard_map/transpose(jvp())/div | solution.py:32
  88.7 1.5 %fusion.45 = (f32[32,32,32]{1,0,2:T(8,128)S(1)}, f32[32,32,32]{1,0,2:T(8,128)S(1)}) fusion(f32[32,32,32]{1,2,0:T(8,128)S(1)} %copy-done.6, f32[32,32,32]{1,2,0:T(8,128)S(1)} %get-tuple-element.40, f32[32,32,32]{1,0,2:T(8,128)S(1)} %copy-done.1, f32[32,32,32]{1,2,0:T(8,128)S(1)} %get-tuple-element.41, f32[32,32,32]{1,0,2:T(8,128)S(1)} %get-tuple-element.16, ...), kind=kLoop, calls=%fused_computation.101 | loop fusion | flops 524288 | bytes 1048576 | tf_op jit(solution)/shard_map/transpose(jvp())/div | solution.py:32
  90.2 0.8 fusion.43
  91.1 0.8 fusion.39
  93.3 0.8 fusion.31
  94.3 1.1 copy.177
  95.4 11.1 %fusion.156 = f32[1024,4,3]{1,2,0:T(4,128)} fusion(f32[1024,4,8]{2,1,0:T(4,128)S(1)} %copy.177, f32[8,3,1024]{1,0,2:T(8,128)} %copy.146), kind=kOutput, calls=%fused_computation.323 | convolution fusion | flops 1179648 | bytes 278528 | tf_op jit(solution)/shard_map/transpose(jvp(scp,tcp->pst))/dot_general | solution.py:53
  106.5 1.8 %copy.179 = f32[1024,4,3]{0,1,2:T(4,128)S(1)} copy(f32[1024,4,3]{1,2,0:T(4,128)} %fusion.156) | data formatting | bytes 98304 | tf_op jit(solution)/shard_map/transpose(jvp(scp,tcp->pst))/dot_general | solution.py:53
  108.5 16.2 %all-reduce.63 = f32[4,3,1024]{2,1,0:T(4,128)S(1)} all-reduce(f32[4,3,1024]{2,1,0:T(4,128)S(1)} %copy.189), channel_id=2, replica_groups=mesh['tgt'=4,'sup'=8] {'tgt'}, use_global_device_ids=true, to_apply=%region_7.8.clone | all-reduce | flops 12288 | bytes 98304
  (92 shorter events, 10.6 us)
Async XLA Ops:
  0.6 65.7 %copy-start = (f32[4,100]{1,0:T(4,128)S(1)}, f32[4,100]{1,0:T(4,128)}, u32[]{:S(2)}) copy-start(f32[4,100]{1,0:T(4,128)} %param.5) | copy-start | bytes 4804
  1.9 80.8 %all-to-all-start = ((f32[8,1,100]{2,1,0:T(1,128)}), f32[8,1,100]{2,1,0:T(1,128)S(1)}, u32[]{:S(2)}, u32[]{:S(2)}) async-start(f32[8,1,100]{2,1,0:T(1,128)} %concatenate.3), calls=%async_computation | async-start | bytes 8192 | tf_op jit(solution)/shard_map/all_to_all | solution.py:16
  23.5 2.7 %copy-start.19 = (f32[1,3,1024]{2,0,1:T(1,128)S(1)}, f32[1,3,1024]{2,0,1:T(1,128)}, u32[]{:S(2)}) copy-start(f32[1,3,1024]{2,0,1:T(1,128)} %param.4) | copy-start | bytes 36868
  34.5 0.6 copy-start.8
  36.7 13.4 %copy-start.10 = (f32[32,32,4]{1,0,2:T(8,128)}, f32[32,32,4]{1,0,2:T(8,128)S(1)}, u32[]{:S(2)}) copy-start(f32[32,32,4]{1,0,2:T(8,128)S(1)} %get-tuple-element.29) | copy-start | bytes 49156
  50.0 4.2 %copy-start.14 = (f32[32,32,4]{1,2,0:T(4,128)S(1)}, f32[32,32,4]{1,2,0:T(4,128)}, u32[]{:S(2)}) copy-start(f32[32,32,4]{1,2,0:T(4,128)} %copy.152) | copy-start | bytes 49156
  51.1 3.2 %copy-start.12 = (f32[32,32,4]{1,0,2:T(8,128)}, f32[32,32,4]{1,0,2:T(8,128)S(1)}, u32[]{:S(2)}) copy-start(f32[32,32,4]{1,0,2:T(8,128)S(1)} %get-tuple-element.25) | copy-start | bytes 49156
  51.1 3.1 %copy-start.16 = (f32[32,32,4]{1,2,0:T(4,128)}, f32[32,32,4]{1,2,0:T(4,128)S(1)}, u32[]{:S(2)}) copy-start(f32[32,32,4]{1,2,0:T(4,128)S(1)} %copy.160) | copy-start | bytes 49156
  53.4 1.0 copy-start.18
  54.3 6.1 %copy-start.2 = (f32[32,32,32]{1,2,0:T(8,128)}, f32[32,32,32]{1,2,0:T(8,128)S(1)}, u32[]{:S(2)}) copy-start(f32[32,32,32]{1,2,0:T(8,128)S(1)} %get-tuple-element.42) | copy-start | bytes 393220
  54.3 6.1 %copy-start.4 = (f32[32,32,32]{1,2,0:T(8,128)}, f32[32,32,32]{1,2,0:T(8,128)S(1)}, u32[]{:S(2)}) copy-start(f32[32,32,32]{1,2,0:T(8,128)S(1)} %get-tuple-element.43) | copy-start | bytes 393220
  85.3 1.5 %copy-start.3 = (f32[32,32,32]{1,2,0:T(8,128)S(1)}, f32[32,32,32]{1,2,0:T(8,128)}, u32[]{:S(2)}) copy-start(f32[32,32,32]{1,2,0:T(8,128)} %copy-done.2) | copy-start | bytes 393220
  85.3 1.5 %copy-start.5 = (f32[32,32,32]{1,2,0:T(8,128)S(1)}, f32[32,32,32]{1,2,0:T(8,128)}, u32[]{:S(2)}) copy-start(f32[32,32,32]{1,2,0:T(8,128)} %copy-done.4) | copy-start | bytes 393220
  85.3 1.5 %copy-start.7 = (f32[32,32,32]{1,2,0:T(8,128)S(1)}, f32[32,32,32]{1,2,0:T(8,128)}, u32[]{:S(2)}) copy-start(f32[32,32,32]{1,2,0:T(8,128)} %broadcast_bitcast_fusion.1) | copy-start | bytes 393220
  86.8 1.9 %copy-start.1 = (f32[32,32,32]{1,0,2:T(8,128)S(1)}, f32[32,32,32]{1,0,2:T(8,128)}, u32[]{:S(2)}) copy-start(f32[32,32,32]{1,0,2:T(8,128)} %get-tuple-element.27) | copy-start | bytes 393220
  86.8 1.9 %copy-start.6 = (f32[32,32,32]{1,2,0:T(8,128)S(1)}, f32[32,32,32]{1,2,0:T(8,128)}, u32[]{:S(2)}) copy-start(f32[32,32,32]{1,2,0:T(8,128)} %broadcast_bitcast_fusion) | copy-start | bytes 393220
  88.7 1.6 %copy-start.15 = (f32[32,32,4]{1,2,0:T(4,128)S(1)}, f32[32,32,4]{1,2,0:T(4,128)}, u32[]{:S(2)}) copy-start(f32[32,32,4]{1,2,0:T(4,128)} %copy.152) | copy-start | bytes 49156
  88.7 2.4 %copy-start.17 = (f32[32,32,4]{1,2,0:T(4,128)S(1)}, f32[32,32,4]{1,2,0:T(4,128)}, u32[]{:S(2)}) copy-start(f32[32,32,4]{1,2,0:T(4,128)} %copy-done.16) | copy-start | bytes 49156
  90.2 1.8 %copy-start.13 = (f32[32,32,4]{1,0,2:T(8,128)S(1)}, f32[32,32,4]{1,0,2:T(8,128)}, u32[]{:S(2)}) copy-start(f32[32,32,4]{1,0,2:T(8,128)} %copy-done.12) | copy-start | bytes 49156
  90.2 2.1 %copy-start.11 = (f32[32,32,4]{1,0,2:T(8,128)S(1)}, f32[32,32,4]{1,0,2:T(8,128)}, u32[]{:S(2)}) copy-start(f32[32,32,4]{1,0,2:T(8,128)} %copy-done.10) | copy-start | bytes 49156
  106.5 1.8 %copy-start.9 = (f32[4,3,1024]{2,1,0:T(4,128)S(1)}, f32[4,3,1024]{2,1,0:T(4,128)}, u32[]{:S(2)}) copy-start(f32[4,3,1024]{2,1,0:T(4,128)} %copy-done.8) | copy-start | bytes 147460
